TPU v7x, 32 devices: a whole 2x2x4 slice. The times are simulated.
32 devices in a mesh: dp: 16 (over z, y, x), mp: 2 (over core).
Axes of the slice: x: 2, y: 2, z: 4, core: 2. Of those that a mesh axis runs over, the one named last changes fastest.
Arguments:
- head_out: bfloat16 [3, 2048, 4096], P(None, 'dp', 'mp'), may hold values from -6 to 6
- residual: bfloat16 [3, 2048, 4096], P(None, 'dp', 'mp'), may hold values from -6 to 6
- out_weight: bfloat16 [4096, 4096], P('dp', 'mp'), may hold values from -0.09375 to 0.09375
- strategy_table: bfloat16 [64, 4096], P(None, 'mp'), may hold values from -3 to 3
- meta_graph: int32 [64, 64], replicated, may hold values from 0 to 3, as said below
- strategy_ids: int32 [3, 2048], P(None, 'dp'), may hold values from 0 to 63
- cotangent: bfloat16 [3, 2048, 4096], P(None, 'dp', 'mp'), may hold values from -6 to 6
Outputs:
- layer_out: bfloat16 [3, 2048, 4096], P(None, 'dp', 'mp')
- head_grad: bfloat16 [3, 2048, 4096], P(None, 'dp', 'mp')
- weight_grad: float32 [4096, 4096], P('dp', 'mp')
- table_grad: float32 [64, 4096], P(None, 'mp')
Inputs may be any that keep to these rules, and one draw needn't show every extreme that they name: `meta_graph`: entries are zero on and above the diagonal; the last strategy meets the first with weight 3.
All inputs are finite; a program needn't handle non-finite values.
Results may differ from a plain program's by a relative error of at most 0.009.
Values may be sent and summed in bfloat16 or wider, within the bound.
A program may use at most 192 MiB of HBM per device.

v0:
```python
import math
import jax
import jax.numpy as jnp
from jax import lax
from jax.sharding import PartitionSpec as P


def mixture(meta_graph):
    counts = meta_graph.astype(jnp.float32)
    totals = jnp.maximum(jnp.sum(counts, axis=1, keepdims=True), 1.0)
    return jnp.eye(meta_graph.shape[0], dtype=jnp.float32) + counts / totals


def on_device(head_out, residual, out_weight, strategy_table, meta_graph, strategy_ids, cotangent):
    highest = lax.Precision.HIGHEST
    batches, local_rows, head_cols = head_out.shape
    strategies = meta_graph.shape[0]
    mixing = mixture(meta_graph)
    table = jnp.dot(mixing, strategy_table.astype(jnp.float32), precision=highest)
    grad_scale = 1.0 / math.sqrt(batches * local_rows * lax.axis_size("dp"))
    model_width = out_weight.shape[0] * lax.axis_size("dp")
    full_weight = lax.all_gather(out_weight, "dp", axis=0, tiled=True)
    weight_acc = jnp.zeros((model_width, head_cols), jnp.float32)
    table_acc = jnp.zeros(table.shape, jnp.float32)
    outputs = []
    head_grads = []
    for batch in range(batches):
        current = head_out[batch]
        partial_sum = lax.dot_general(
            current, full_weight, (((1,), (1,)), ((), ())), preferred_element_type=jnp.float32
        )
        projected = lax.psum_scatter(
            partial_sum.astype(jnp.bfloat16), "mp", scatter_dimension=1, tiled=True
        ).astype(jnp.float32)
        one_hot = (
            strategy_ids[batch][:, None] == lax.broadcasted_iota(jnp.int32, (1, strategies), 1)
        ).astype(jnp.float32)
        gating = 1.0 + jnp.dot(one_hot, table, precision=highest)
        outputs.append(
            (residual[batch].astype(jnp.float32) + projected * gating).astype(jnp.bfloat16)
        )
        grad_local = (cotangent[batch].astype(jnp.float32) * gating).astype(jnp.bfloat16)
        full_grad = lax.all_gather(grad_local, "mp", axis=1, tiled=True)
        head_grad = jnp.dot(full_grad, full_weight, preferred_element_type=jnp.float32)
        head_grads.append(head_grad.astype(jnp.bfloat16))
        cond_grad = cotangent[batch].astype(jnp.float32) * projected
        table_acc = table_acc + lax.dot_general(
            one_hot,
            cond_grad,
            (((0,), (0,)), ((), ())),
            precision=highest,
            preferred_element_type=jnp.float32,
        )
        if batch + 1 < batches:
            weight_acc = weight_acc + lax.dot_general(
                full_grad, current, (((0,), (0,)), ((), ())), preferred_element_type=jnp.float32
            )
    weight_acc = weight_acc + lax.dot_general(
        full_grad, current, (((0,), (0,)), ((), ())), preferred_element_type=jnp.float32
    )
    weight_sum = lax.psum_scatter(weight_acc, "dp", scatter_dimension=0, tiled=True)
    table_sum = lax.psum(table_acc, "dp")
    table_grad = jnp.dot(mixing.T, table_sum, precision=highest) * grad_scale
    return (jnp.stack(outputs), jnp.stack(head_grads), weight_sum * grad_scale, table_grad)


def solution(mesh):
    placed = (
        P(None, "dp", "mp"),
        P(None, "dp", "mp"),
        P("dp", "mp"),
        P(None, "mp"),
        P(),
        P(None, "dp"),
        P(None, "dp", "mp"),
    )
    return jax.shard_map(
        on_device,
        mesh=mesh,
        in_specs=placed,
        out_specs=(P(None, "dp", "mp"), P(None, "dp", "mp"), P("dp", "mp"), P(None, "mp")),
        check_vma=False,
    )
```

profile of v0, /device:TPU:10, one launch (start us, length us, event | category | flops | bytes accessed | tf_op | source)
XLA Modules:
  0.0 1102.9 jit_solution(4540015493611375227)
XLA Ops:
  8.0 193.1 %all-gather.5.cloned.1.call-done = bf16[4096,2048]{1,0:T(8,128)(2,1)} async-done(((bf16[256,2048]{1,0:T(8,128)(2,1)}), bf16[4096,2048]{1,0:T(8,128)(2,1)}) %all-gather.5.cloned.1.call-update) | async-done | bytes 16777232 | tf_op jit(solution)/shard_map/all_gather | solution.py:22
  201.1 12.6 %convolution_convert_fusion = bf16[128,4096]{1,0:T(8,128)(2,1)} fusion(bf16[4096,2048]{1,0:T(8,128)(2,1)} %all-gather.5.cloned.1.call-done, bf16[3,128,2048]{2,1,0:T(8,128)(2,1)} %param.7), kind=kOutput, calls=%fused_computation.1 | convolution fusion | flops 2148007936 | bytes 18350080 | tf_op jit(solution)/shard_map/dot_general | solution.py:29
  213.7 12.4 %convolution_convert_fusion.1 = bf16[128,4096]{1,0:T(8,128)(2,1)} fusion(bf16[4096,2048]{1,0:T(8,128)(2,1)} %all-gather.5.cloned.1.call-done, bf16[3,128,2048]{2,1,0:T(8,128)(2,1)S(1)} %copy-done.5), kind=kOutput, calls=%fused_computation.2 | convolution fusion | flops 2148007936 | bytes 18350080 | tf_op jit(solution)/shard_map/dot_general | solution.py:29
  226.2 12.4 %convolution_convert_fusion.2 = bf16[128,4096]{1,0:T(8,128)(2,1)} fusion(bf16[4096,2048]{1,0:T(8,128)(2,1)} %all-gather.5.cloned.1.call-done, bf16[3,128,2048]{2,1,0:T(8,128)(2,1)S(1)} %copy-done.5), kind=kOutput, calls=%fused_computation.3 | convolution fusion | flops 2148007936 | bytes 18350080 | tf_op jit(solution)/shard_map/dot_general | solution.py:29
  240.0 1.6 convolution_add_fusion.1
  241.6 6.3 reduce-scatter.5.cloned.1.call-done
  247.9 5.1 fusion.15
  254.4 1.9 fusion.10
  256.3 1.7 convolution_add_fusion.4
  258.1 2.5 convolution_add_fusion.3
  260.6 2.8 all-gather.9.cloned.1.call-done
  263.4 15.0 %fusion.21 = f32[4096,2048]{1,0:T(8,128)} fusion(bf16[128,4096]{1,0:T(8,128)(2,1)} %all-gather.9.cloned.1.call-done, bf16[3,128,2048]{2,1,0:T(8,128)(2,1)S(1)} %copy-done.5), kind=kOutput, calls=%fused_computation.46 | convolution fusion | flops 2147483648 | bytes 35127296 | tf_op jit(solution)/shard_map/dot_general | solution.py:55
  278.4 14.7 %fusion.24 = f32[4096,2048]{1,0:T(8,128)} fusion(bf16[128,4096]{1,0:T(8,128)(2,1)} %all-gather.7.cloned.1.call-done, bf16[3,128,2048]{2,1,0:T(8,128)(2,1)S(1)} %copy-done.5), kind=kOutput, calls=%fused_computation.49 | convolution fusion | flops 2147483648 | bytes 35127296 | tf_op jit(solution)/shard_map/dot_general | solution.py:55
  293.1 34.7 %add_add_fusion = f32[4096,2048]{1,0:T(8,128)} fusion(f32[4096,2048]{1,0:T(8,128)} %fusion.24, f32[4096,2048]{1,0:T(8,128)} %fusion.21, bf16[128,4096]{1,0:T(8,128)(2,1)} %all-gather.11.cloned.1.call-done, bf16[3,128,2048]{2,1,0:T(8,128)(2,1)S(1)} %copy-done.5), kind=kOutput, calls=%fused_computation | convolution fusion | flops 2164260864 | bytes 102236160 | tf_op jit(solution)/shard_map/dot_general | solution.py:58
  327.9 1.0 copy-done.8
  329.2 1.3 pad_maximum_fusion
  330.5 71.3 %all-reduce.2.cloned.1.call-done = f32[64,2048]{1,0:T(8,128)} async-done(((f32[64,2048]{1,0:T(8,128)}), f32[64,2048]{1,0:T(8,128)}) %all-reduce.2.cloned.1.call-update) | async-done | bytes 524304 | tf_op jit(solution)/shard_map/psum | solution.py:62
  401.9 2.5 convolution_multiply_fusion
  404.4 8.3 fusion
  412.8 9.0 fusion.2
  421.9 2.5 fusion.1
  424.4 1.3 pad_maximum_fusion.1
  425.7 667.4 %reduce-scatter.11.cloned.1.call-done = f32[256,2048]{1,0:T(8,128)} async-done(((f32[4096,2048]{1,0:T(8,128)}), f32[256,2048]{1,0:T(8,128)}) %reduce-scatter.11.cloned.1.call-update) | async-done | bytes 2097168 | tf_op jit(solution)/shard_map/reduce_scatter | solution.py:61
  1093.1 3.2 broadcast_multiply_fusion
  (61 shorter events, 4.1 us)
Async XLA Ops:
  7.2 231.8 %copy-start = (bf16[64,2048]{1,0:T(8,128)(2,1)S(1)}, bf16[64,2048]{1,0:T(8,128)(2,1)}, u32[]{:S(2)}) copy-start(bf16[64,2048]{1,0:T(8,128)(2,1)} %param.10) | copy-start | bytes 786436
  7.2 193.9 %all-gather.5.cloned.1.call-start = ((), (), s32[]{:S(2)}) async-start(), calls=%async_computation.4 | async-start | bytes 17825792 | tf_op jit(solution)/shard_map/all_gather | solution.py:22
  7.9 205.8 %copy-start.5 = (bf16[3,128,2048]{2,1,0:T(8,128)(2,1)S(1)}, bf16[3,128,2048]{2,1,0:T(8,128)(2,1)}, u32[]{:S(2)}) copy-start(bf16[3,128,2048]{2,1,0:T(8,128)(2,1)} %param.7) | copy-start | bytes 4718596
  7.9 233.7 %reduce-scatter.9.cloned.1.call-start = ((), (), s32[]{:S(2)}) async-start(), calls=%async_computation.7 | async-start | bytes 1572864 | tf_op jit(solution)/shard_map/reduce_scatter | solution.py:32
  213.7 28.0 %reduce-scatter.7.cloned.1.call-start = ((), (), s32[]{:S(2)}) async-start(), calls=%async_computation.6 | async-start | bytes 1572864 | tf_op jit(solution)/shard_map/reduce_scatter | solution.py:32
  226.1 12.7 %copy-start.11 = (s32[64,64]{1,0:T(8,128)S(1)}, s32[64,64]{1,0:T(8,128)}, u32[]{:S(2)}) copy-start(s32[64,64]{1,0:T(8,128)} %param.11) | copy-start | bytes 49156
  226.1 12.8 %copy-start.12 = (s32[3,128]{1,0:T(4,128)S(1)}, s32[3,128]{1,0:T(4,128)}, u32[]{:S(2)}) copy-start(s32[3,128]{1,0:T(4,128)} %param.12) | copy-start | bytes 4612
  226.1 21.8 %reduce-scatter.5.cloned.1.call-start = ((), (), s32[]{:S(2)}) async-start(), calls=%async_computation.5 | async-start | bytes 1572864 | tf_op jit(solution)/shard_map/reduce_scatter | solution.py:32
  238.6 24.8 %all-gather.9.cloned.1.call-start = ((), (), s32[]{:S(2)}) async-start(), calls=%async_computation.9 | async-start | bytes 1572864 | tf_op jit(solution)/shard_map/all_gather | solution.py:43
  253.0 3.3 copy-start.7
  253.1 25.3 %all-gather.7.cloned.1.call-start = ((), (), s32[]{:S(2)}) async-start(), calls=%async_computation.8 | async-start | bytes 1572864 | tf_op jit(solution)/shard_map/all_gather | solution.py:43
  253.7 39.5 %all-gather.11.cloned.1.call-start = ((), (), s32[]{:S(2)}) async-start(), calls=%async_computation.10 | async-start | bytes 1572864 | tf_op jit(solution)/shard_map/all_gather | solution.py:43
  253.7 4.3 copy-start.6
  254.4 147.5 %all-reduce.2.cloned.1.call-start = ((), (), s32[]{:S(2)}) async-start(), calls=%async_computation.12 | async-start | bytes 1048576 | tf_op jit(solution)/shard_map/psum | solution.py:62
  260.6 832.5 %reduce-scatter.11.cloned.1.call-start = ((), (), s32[]{:S(2)}) async-start(), calls=%async_computation.11 | async-start | bytes 35651584 | tf_op jit(solution)/shard_map/reduce_scatter | solution.py:61
  327.9 1.4 copy-start.10
  329.2 75.2 %copy-start.3 = (bf16[128,4096]{1,0:T(8,128)(2,1)S(1)}, bf16[128,4096]{1,0:T(8,128)(2,1)}, u32[]{:S(2)}) copy-start(bf16[128,4096]{1,0:T(8,128)(2,1)} %all-gather.7.cloned.1.call-done) | copy-start | bytes 3145732
  404.4 8.3 copy-start.4
  404.4 17.4 %slice-start = ((s8[16777216]{0:T(1024)(128)(4,1)}), s8[4194304]{0:T(1024)(128)(4,1)S(1)}, s32[]{:S(2)}) async-start(s8[16777216]{0:T(1024)(128)(4,1)} %bitcast.80), calls=%async_computation.13 | async-start | bytes 8388608
  404.4 17.4 %slice-start.1 = ((s8[16777216]{0:T(1024)(128)(4,1)}), s8[4194304]{0:T(1024)(128)(4,1)S(1)}, s32[]{:S(2)}) async-start(s8[16777216]{0:T(1024)(128)(4,1)} %bitcast.80), calls=%async_computation.14 | async-start | bytes 8388608
  404.4 17.4 %slice-start.2 = ((s8[16777216]{0:T(1024)(128)(4,1)}), s8[4194304]{0:T(1024)(128)(4,1)S(1)}, s32[]{:S(2)}) async-start(s8[16777216]{0:T(1024)(128)(4,1)} %bitcast.80), calls=%async_computation.15 | async-start | bytes 8388608
  412.8 9.1 slice-start.3
  412.8 9.1 copy-start.2
  424.4 672.0 %copy-start.1 = (bf16[64,2048]{1,0:T(8,128)(2,1)S(1)}, bf16[64,2048]{1,0:T(8,128)(2,1)}, u32[]{:S(2)}) copy-start(bf16[64,2048]{1,0:T(8,128)(2,1)} %param.10) | copy-start | bytes 786436
  (2 other events, 2.2 us)
Sparse Core Ops, SparseCore 0:
  10.8 190.2 all-gather.4
  213.8 8.7 reduce-scatter.8
  226.2 8.9 reduce-scatter.6
  238.7 9.1 reduce-scatter.4
  253.2 10.1 all-gather.8
  264.8 10.1 all-gather.6
  276.6 10.1 all-gather.10
  292.5 109.2 all-reduce.1
  404.2 688.8 reduce-scatter.10
where the time goes:
time: 1100 us
  waiting for transfers between devices  943 us (86%)
  matrix products  138 us (13%)
  between operations  14.1 us (1%)
    reduce_scatter x1, waiting for transfers between devices, on_device(): lax.psum_scatter(weight_acc, 'dp', scatter_dimension=0, tiled=True)  667 us
    all_gather x1, waiting for transfers between devices, on_device(): full_weight = lax.all_gather(out_weight, 'dp', axis=0, tiled=True)  193 us
    psum x1, waiting for transfers between devices, on_device(): table_sum = lax.psum(table_acc, 'dp')  71.3 us
    dot_general x3, matrix products, on_device(): lax.dot_general(full_grad, current, (((0,), (0,)), ((), ())), preferred_e...  64.4 us
    dot_general x3, matrix products, on_device(): lax.dot_general(current, full_weight, (((1,), (1,)), ((), ())), preferred...  37.3 us
  transfers between devices with their start and end apart: 9, of which 5 were waited for; matrix products, arithmetic and copies ran while one was open for 11% of the time, Pallas kernels for 0%

commit v1 on v0

--- a/solution.py
+++ b/solution.py
@@ -19,7 +19,15 @@
     table = jnp.dot(mixing, strategy_table.astype(jnp.float32), precision=highest)
     grad_scale = 1.0 / math.sqrt(batches * local_rows * lax.axis_size("dp"))
     model_width = out_weight.shape[0] * lax.axis_size("dp")
-    full_weight = lax.all_gather(out_weight, "dp", axis=0, tiled=True)
+    full_weight = jnp.concatenate(
+        lax.all_to_all(
+            jnp.stack(lax.axis_size("dp") * [out_weight]),
+            axis_name="dp",
+            concat_axis=0,
+            split_axis=0,
+        ),
+        axis=0,
+    )
     weight_acc = jnp.zeros((model_width, head_cols), jnp.float32)
     table_acc = jnp.zeros(table.shape, jnp.float32)
     outputs = []

time: 1100 us -> 1280 us (1.16)
  blocking collectives: 0 us -> 369 us
  waiting for transfers between devices: 943 us -> 748 us
    all_to_all x0 -> x1, blocking collectives: none -> 369 us  [on_device(): lax.all_to_all(jnp.stack(lax.axis_size('dp') * [out_weight]), axis_name='...]
    all_gather x1 -> x0, waiting for transfers between devices: 193 us -> none  [on_device(): full_weight = lax.all_gather(out_weight, 'dp', axis=0, tiled=True)]
  transfers between devices with their start and end apart: 9 -> 8, of which waited for: 5 -> 4; matrix products, arithmetic and copies ran while one was open for 11% -> 10% of each run, Pallas kernels for 0% -> 0%
where the time goes in v1:
time: 1280 us
  waiting for transfers between devices  748 us (58%)
  blocking collectives  369 us (29%)
  matrix products  138 us (11%)
  between operations  14.4 us (1%)
    reduce_scatter x1, waiting for transfers between devices, on_device(): lax.psum_scatter(weight_acc, 'dp', scatter_dimension=0, tiled=True)  667 us
    all_to_all x1, blocking collectives, on_device(): lax.all_to_all(jnp.stack(lax.axis_size('dp') * [out_weight]), axis_name='...  369 us
    psum x1, waiting for transfers between devices, on_device(): table_sum = lax.psum(table_acc, 'dp')  71.3 us
    dot_general x3, matrix products, on_device(): lax.dot_general(full_grad, current, (((0,), (0,)), ((), ())), preferred_e...  64.3 us
    dot_general x3, matrix products, on_device(): lax.dot_general(current, full_weight, (((1,), (1,)), ((), ())), preferred...  37.3 us
  transfers between devices with their start and end apart: 8, of which 4 were waited for; matrix products, arithmetic and copies ran while one was open for 10% of the time, Pallas kernels for 0%

profile of v1, /device:TPU:10, one launch (start us, length us, event | category | flops | bytes accessed | tf_op | source)
XLA Modules:
  0.0 1281.0 jit_solution(14918082927766021620)
XLA Ops:
  7.2 3.9 stack.18
  11.1 369.1 %all_to_all.5 = bf16[16,256,2048]{2,1,0:T(8,128)(2,1)} all-to-all(bf16[16,256,2048]{2,1,0:T(8,128)(2,1)S(1)} %stack.18), channel_id=1, replica_groups=mesh['dp'=16,'mp'=2] {'dp'}, dimensions={0} | all-to-all | bytes 33554432 | tf_op jit(solution)/shard_map/all_to_all | solution.py:23
  380.2 12.4 convolution_convert_fusion
  392.7 12.4 convolution_convert_fusion.1
  405.3 12.5 convolution_convert_fusion.2
  419.1 1.6 convolution_add_fusion.1
  420.7 5.2 reduce-scatter.5.cloned.1.call-done
  425.9 5.1 fusion.15
  432.3 1.9 fusion.10
  434.2 1.7 convolution_add_fusion.4
  435.9 2.5 convolution_add_fusion.3
  438.7 2.7 all-gather.6.cloned.1.call-done
  441.4 14.8 %fusion.21 = f32[4096,2048]{1,0:T(8,128)} fusion(bf16[128,4096]{1,0:T(8,128)(2,1)} %all-gather.6.cloned.1.call-done, bf16[3,128,2048]{2,1,0:T(8,128)(2,1)S(1)} %copy-done.5), kind=kOutput, calls=%fused_computation.46 | convolution fusion | flops 2147483648 | bytes 35127296 | tf_op jit(solution)/shard_map/dot_general | solution.py:63
  456.3 14.7 %fusion.24 = f32[4096,2048]{1,0:T(8,128)} fusion(bf16[128,4096]{1,0:T(8,128)(2,1)} %all-gather.4.cloned.1.call-done, bf16[3,128,2048]{2,1,0:T(8,128)(2,1)S(1)} %copy-done.5), kind=kOutput, calls=%fused_computation.49 | convolution fusion | flops 2147483648 | bytes 35127296 | tf_op jit(solution)/shard_map/dot_general | solution.py:63
  471.0 34.8 %add_add_fusion = f32[4096,2048]{1,0:T(8,128)} fusion(f32[4096,2048]{1,0:T(8,128)} %fusion.24, f32[4096,2048]{1,0:T(8,128)} %fusion.21, bf16[128,4096]{1,0:T(8,128)(2,1)} %all-gather.8.cloned.1.call-done, bf16[3,128,2048]{2,1,0:T(8,128)(2,1)S(1)} %copy-done.5), kind=kOutput, calls=%fused_computation | convolution fusion | flops 2164260864 | bytes 102236160 | tf_op jit(solution)/shard_map/dot_general | solution.py:66
  507.1 1.3 pad_maximum_fusion
  508.4 71.3 %all-reduce.2.cloned.1.call-done = f32[64,2048]{1,0:T(8,128)} async-done(((f32[64,2048]{1,0:T(8,128)}), f32[64,2048]{1,0:T(8,128)}) %all-reduce.2.cloned.1.call-update) | async-done | bytes 524304 | tf_op jit(solution)/shard_map/psum | solution.py:70
  579.8 2.5 convolution_multiply_fusion
  582.3 8.3 fusion
  590.7 9.0 fusion.2
  599.7 2.5 fusion.1
  602.3 1.3 pad_maximum_fusion.1
  603.6 667.4 %reduce-scatter.11.cloned.1.call-done = f32[256,2048]{1,0:T(8,128)} async-done(((f32[4096,2048]{1,0:T(8,128)}), f32[256,2048]{1,0:T(8,128)}) %reduce-scatter.11.cloned.1.call-update) | async-done | bytes 2097168 | tf_op jit(solution)/shard_map/reduce_scatter | solution.py:69
  1271.0 3.2 broadcast_multiply_fusion
  (60 shorter events, 4.4 us)
Async XLA Ops:
  7.2 410.9 %copy-start = (bf16[64,2048]{1,0:T(8,128)(2,1)S(1)}, bf16[64,2048]{1,0:T(8,128)(2,1)}, u32[]{:S(2)}) copy-start(bf16[64,2048]{1,0:T(8,128)(2,1)} %param.10) | copy-start | bytes 786436
  7.2 413.6 %reduce-scatter.9.cloned.1.call-start = ((), (), s32[]{:S(2)}) async-start(), calls=%async_computation.7 | async-start | bytes 1572864 | tf_op jit(solution)/shard_map/reduce_scatter | solution.py:40
  11.1 369.1 %copy-start.5 = (bf16[3,128,2048]{2,1,0:T(8,128)(2,1)S(1)}, bf16[3,128,2048]{2,1,0:T(8,128)(2,1)}, u32[]{:S(2)}) copy-start(bf16[3,128,2048]{2,1,0:T(8,128)(2,1)} %param.7) | copy-start | bytes 4718596
  392.6 28.1 %reduce-scatter.7.cloned.1.call-start = ((), (), s32[]{:S(2)}) async-start(), calls=%async_computation.6 | async-start | bytes 1572864 | tf_op jit(solution)/shard_map/reduce_scatter | solution.py:40
  405.1 12.8 %copy-start.11 = (s32[64,64]{1,0:T(8,128)S(1)}, s32[64,64]{1,0:T(8,128)}, u32[]{:S(2)}) copy-start(s32[64,64]{1,0:T(8,128)} %param.11) | copy-start | bytes 49156
  405.1 12.9 %copy-start.12 = (s32[3,128]{1,0:T(4,128)S(1)}, s32[3,128]{1,0:T(4,128)}, u32[]{:S(2)}) copy-start(s32[3,128]{1,0:T(4,128)} %param.12) | copy-start | bytes 4612
  405.1 20.8 %reduce-scatter.5.cloned.1.call-start = ((), (), s32[]{:S(2)}) async-start(), calls=%async_computation.5 | async-start | bytes 1572864 | tf_op jit(solution)/shard_map/reduce_scatter | solution.py:40
  417.9 23.6 %all-gather.6.cloned.1.call-start = ((), (), s32[]{:S(2)}) async-start(), calls=%async_computation.9 | async-start | bytes 1572864 | tf_op jit(solution)/shard_map/all_gather | solution.py:51
  431.1 3.1 copy-start.7
  431.1 25.2 %all-gather.4.cloned.1.call-start = ((), (), s32[]{:S(2)}) async-start(), calls=%async_computation.8 | async-start | bytes 1572864 | tf_op jit(solution)/shard_map/all_gather | solution.py:51
  431.7 39.3 %all-gather.8.cloned.1.call-start = ((), (), s32[]{:S(2)}) async-start(), calls=%async_computation.10 | async-start | bytes 1572864 | tf_op jit(solution)/shard_map/all_gather | solution.py:51
  431.7 4.2 copy-start.6
  432.3 147.5 %all-reduce.2.cloned.1.call-start = ((), (), s32[]{:S(2)}) async-start(), calls=%async_computation.12 | async-start | bytes 1048576 | tf_op jit(solution)/shard_map/psum | solution.py:70
  438.4 832.5 %reduce-scatter.11.cloned.1.call-start = ((), (), s32[]{:S(2)}) async-start(), calls=%async_computation.11 | async-start | bytes 35651584 | tf_op jit(solution)/shard_map/reduce_scatter | solution.py:69
  505.7 1.2 copy-start.9
  505.7 1.4 copy-start.10
  507.1 75.2 %copy-start.3 = (bf16[128,4096]{1,0:T(8,128)(2,1)S(1)}, bf16[128,4096]{1,0:T(8,128)(2,1)}, u32[]{:S(2)}) copy-start(bf16[128,4096]{1,0:T(8,128)(2,1)} %all-gather.4.cloned.1.call-done) | copy-start | bytes 3145732
  582.3 8.3 copy-start.4
  582.3 17.4 %slice-start = ((s8[16777216]{0:T(1024)(128)(4,1)}), s8[4194304]{0:T(1024)(128)(4,1)S(1)}, s32[]{:S(2)}) async-start(s8[16777216]{0:T(1024)(128)(4,1)} %bitcast.86), calls=%async_computation.13 | async-start | bytes 8388608
  582.3 17.4 %slice-start.1 = ((s8[16777216]{0:T(1024)(128)(4,1)}), s8[4194304]{0:T(1024)(128)(4,1)S(1)}, s32[]{:S(2)}) async-start(s8[16777216]{0:T(1024)(128)(4,1)} %bitcast.86), calls=%async_computation.14 | async-start | bytes 8388608
  582.3 17.4 %slice-start.2 = ((s8[16777216]{0:T(1024)(128)(4,1)}), s8[4194304]{0:T(1024)(128)(4,1)S(1)}, s32[]{:S(2)}) async-start(s8[16777216]{0:T(1024)(128)(4,1)} %bitcast.86), calls=%async_computation.15 | async-start | bytes 8388608
  590.6 9.1 slice-start.3
  590.6 9.1 copy-start.2
  602.2 671.9 %copy-start.1 = (bf16[64,2048]{1,0:T(8,128)(2,1)S(1)}, bf16[64,2048]{1,0:T(8,128)(2,1)}, u32[]{:S(2)}) copy-start(bf16[64,2048]{1,0:T(8,128)(2,1)} %param.10) | copy-start | bytes 786436
  (1 other events, 1.0 us)
Sparse Core Ops, SparseCore 0:
  392.7 8.0 reduce-scatter.8
  405.2 8.0 reduce-scatter.6
  418.0 7.9 reduce-scatter.4
  431.2 10.1 all-gather.5
  442.8 10.1 all-gather.3
  454.5 10.1 all-gather.7
  470.4 109.2 all-reduce.1
  582.1 688.8 reduce-scatter.10
